TPU v7x, 32 devices: a whole 2x2x4 slice. The times are simulated.
32 devices in a mesh: groups: 2 (over y), tile: 4 (over z), sub: 2 (over x), rep: 2 (over core).
Axes of the slice: x: 2, y: 2, z: 4, core: 2. Of those that a mesh axis runs over, the one named last changes fastest.
Arguments:
- pressure: float32 [64, 32, 256], P(('groups', 'tile'), 'sub', 'rep'), parts along dimension 0, may hold values from -3 to 3
- previous_pressure: float32 [64, 32, 256], P(('groups', 'tile'), 'sub', 'rep'), parts along dimension 0, may hold values from -3 to 3
- courant_square: float32 [64, 32, 256], P(('groups', 'tile'), 'sub', 'rep'), parts along dimension 0, may hold values from 0.07 to 0.22
- node_area: float32 [12288], P(('groups', 'tile', 'sub', 'rep')), parts along dimension 0, may hold values from 0.25 to 4
- mode_shapes: bfloat16 [12288, 2048], P(('groups', 'tile', 'sub', 'rep')), parts along dimension 0, may hold values from -0.049804688 to 0.049804688
- frequency: float32 [4096], P('groups'), parts along dimension 0, may hold values from 0.4 to 1.3
- damping_ratio: float32 [4096], P('groups'), parts along dimension 0, may hold values from 0.02 to 0.4
- modal_start: float32 [2, 4096], P(None, 'groups'), parts along dimension 1, may hold values from -4 to 4
- slot_cell: int32 [8, 2, 2, 384], P(('groups', 'tile'), 'sub', 'rep'), parts along dimension 0, may hold values from 0 to 16383, as said below
- slot_owner: int32 [8, 2, 2, 384, 1], P(('groups', 'tile'), 'sub', 'rep'), parts along dimension 0, may hold values from 0 to 3; in each aligned block of 384 rows (0 to 383, 384 to 767, ..., all dimensions but the last counted through in order) at most 96 rows name the same one
- surface_count: int32 [4, 2, 4], P(('groups', 'sub'), 'rep', 'tile'), parts along dimension 0, may hold values from 1 to 384, 512 in all within a row
Outputs:
- final_pressure: float32 [64, 32, 256], P(('groups', 'tile'), 'sub', 'rep'), parts along dimension 0
- prior_pressure: float32 [64, 32, 256], P(('groups', 'tile'), 'sub', 'rep'), parts along dimension 0
- surface_accel: bfloat16 [8, 2, 2, 4, 384], P(('groups', 'tile'), 'sub', 'rep'), parts along dimension 0
- modal_state: float32 [2, 4096], P(None, ('groups', 'tile', 'sub', 'rep')), parts along dimension 1
There are 2 independent parts, one for each index of `groups`. A program takes and returns all parts, laid end to end along the dimension named above; each array names one. Nothing has to cross between parts.
Inputs may be any that keep to these rules, and one draw needn't show every extreme that they name: `slot_cell`: slot j of a block lies in the block's cells j * (42) to (j + 1) (42) - 1, so a block's slots name distinct cells. `slot_owner`: every owner index is named by exactly 96 of the 384 slots of each block (t, s, r). `surface_count`: for fixed s and r the counts over t sum to 128 times the number of tile indices, and one of them equals 384.
All inputs are finite; a program needn't handle non-finite values. No bound on the sum of `surface_count` on one device may be relied on, other than what follows from the above.
Results may differ from a plain program's by a relative error of at most 0.0098.
Values may be sent and summed in bfloat16 or wider, within the bound.
A program may use at most 64 MiB of HBM per device.

v0:
```python
import jax
import jax.numpy as jnp
from jax import lax
from jax.sharding import PartitionSpec as P

STEPS = 4
HALO = 4
nonlinear = 0.03
viscous = 0.02


def extended(shard, sides, width):
    for axis, dim in sides:
        count, length = (lax.axis_size(axis), shard.shape[dim])
        up = [(i, (i + 1) % count) for i in range(count - 1)]
        down = [(j, i) for i, j in up]
        last = lax.slice_in_dim(shard, length - width, length, axis=dim)
        first = lax.slice_in_dim(shard, 0, width, axis=dim)
        before = lax.ppermute(last, axis, up)
        after = lax.ppermute(first, axis, down)
        shard = jnp.concatenate([before, shard, after], axis=dim)
    return shard


def laplace(padded):
    middle = padded[1:-1, 1:-1, 1:-1]
    summed = padded[2:, 1:-1, 1:-1] + padded[:-2, 1:-1, 1:-1]
    summed = summed + padded[1:-1, 2:, 1:-1] + padded[1:-1, :-2, 1:-1]
    summed = summed + padded[1:-1, 1:-1, 2:] + padded[1:-1, 1:-1, :-2]
    return summed - 6.0 * middle


def advance(wide_now, wide_before, coefficient):
    current = wide_now[1:-1, 1:-1, 1:-1]
    before = wide_before[1:-1, 1:-1, 1:-1]
    change = current - before
    driving = (
        coefficient * laplace(wide_now)
        + viscous * laplace(wide_now - wide_before)
        + 2.0 * nonlinear * change * change
    )
    return 2.0 * current - before + (1.0 + 2.0 * nonlinear * current) * driving


def routing(owners, live_count, tile_total):
    slot_total = owners.shape[0]
    bucket = slot_total // tile_total
    position = jnp.arange(slot_total, dtype=jnp.int32)
    is_live = position < live_count
    member = (
        (owners[:, None] == jnp.arange(tile_total, dtype=jnp.int32)[None, :]) & is_live[:, None]
    ).astype(jnp.float32)
    earlier = (position[None, :] < position[:, None]).astype(jnp.float32)
    before = jnp.dot(earlier, member, precision=lax.Precision.HIGHEST)
    bucket_rank = jnp.sum(before * member, axis=1).astype(jnp.int32)
    target = owners * bucket + bucket_rank
    return ((target[:, None] == position[None, :]) & is_live[:, None]).astype(jnp.bfloat16)


def oscillate(forces, frequency, damping_ratio, start_state):

    def advance_mode(carried, force_row):
        displace, velocity = carried
        acceleration = (
            force_row
            - 2.0 * damping_ratio * frequency * velocity
            - frequency * frequency * displace
        )
        velocity = velocity + acceleration
        displace = displace + velocity
        return ((displace, velocity), acceleration)

    (displace, velocity), modal_accel = lax.scan(
        advance_mode, (start_state[0], start_state[1]), forces
    )
    return (modal_accel, jnp.stack([displace, velocity]))


def trim_rim(array, depth):
    return array[
        depth : array.shape[0] - depth,
        depth : array.shape[1] - depth,
        depth : array.shape[2] - depth,
    ]


def inside_range(offset, length, axis_devices, margin):
    position = offset * length - margin + jnp.arange(length + 2 * margin, dtype=jnp.int32)
    return ((position >= 0) & (position < axis_devices * length)).astype(jnp.float32)


def body(
    pressure,
    previous_pressure,
    courant_square,
    node_area,
    mode_shapes,
    frequency,
    damping_ratio,
    modal_start,
    slot_cell,
    slot_owner,
    surface_count,
):
    tile_total = lax.axis_size("tile")
    extent_first, extent_second, extent_third = pressure.shape
    slot_total = slot_cell.shape[-1]
    bucket = slot_total // tile_total
    routing_matrix = routing(slot_owner.reshape(slot_total), surface_count.reshape(()), tile_total)
    cell_index = slot_cell.reshape(slot_total)
    fields = jnp.stack([pressure, previous_pressure])
    margin = HALO
    coef_wide = extended(courant_square, (("tile", 0), ("sub", 1), ("rep", 2)), margin)
    inside_first = inside_range(lax.axis_index("tile"), extent_first, lax.axis_size("tile"), margin)
    inside_second = inside_range(lax.axis_index("sub"), extent_second, lax.axis_size("sub"), margin)
    inside_third = inside_range(lax.axis_index("rep"), extent_third, lax.axis_size("rep"), margin)
    inside = (
        inside_first[:, None, None] * inside_second[None, :, None] * inside_third[None, None, :]
    )

    def deep_block(carried, unused):
        padded = extended(carried, (("tile", 1), ("sub", 2), ("rep", 3)), margin)
        recorded = []
        for layer_index in range(margin):
            edge_depth = layer_index + 1
            updated = advance(padded[0], padded[1], trim_rim(coef_wide, edge_depth)) * trim_rim(
                inside, edge_depth
            )
            interior = trim_rim(updated, margin - edge_depth)
            recorded.append(jnp.take(interior.reshape(-1), cell_index).astype(jnp.bfloat16))
            padded = jnp.stack([updated, trim_rim(padded[0], 1)])
        return (padded, jnp.stack(recorded))

    fields, history = lax.scan(deep_block, fields, None, length=STEPS // margin)
    history = history.reshape(STEPS, slot_total)
    final_field = fields[0]
    prior_field = fields[1]
    bucketed = jnp.dot(history, routing_matrix, preferred_element_type=jnp.float32).astype(
        jnp.bfloat16
    )
    bucketed = bucketed.reshape(STEPS, tile_total, bucket)
    arrived = lax.all_to_all(bucketed, "tile", split_axis=1, concat_axis=1, tiled=True)
    arrived_flat = arrived.reshape(arrived.shape[0], slot_total)
    weighted = (arrived_flat * node_area).astype(jnp.bfloat16)
    partial_forces = jnp.dot(weighted, mode_shapes, preferred_element_type=jnp.float32)
    device_total = lax.axis_size("tile") * lax.axis_size("sub") * lax.axis_size("rep")
    mode_count = mode_shapes.shape[1]
    mode_share = mode_count // device_total
    first_mode = lax.axis_index(("tile", "sub", "rep")) * mode_share
    forces = lax.psum_scatter(
        partial_forces, ("tile", "sub", "rep"), scatter_dimension=1, tiled=True
    )
    local_frequency = lax.dynamic_slice_in_dim(frequency, first_mode, mode_share, 0)
    local_damping = lax.dynamic_slice_in_dim(damping_ratio, first_mode, mode_share, 0)
    local_start = lax.dynamic_slice_in_dim(modal_start, first_mode, mode_share, 1)
    modal_accel, modal_state = oscillate(forces, local_frequency, local_damping, local_start)
    modal_rounded = modal_accel.astype(jnp.bfloat16)
    node_accel = lax.dot_general(
        lax.all_gather(modal_rounded, ("tile", "sub", "rep"), axis=1, tiled=True),
        mode_shapes,
        (((1,), (1,)), ((), ())),
        preferred_element_type=jnp.float32,
    )
    outgoing = node_accel.astype(jnp.bfloat16).reshape(STEPS, tile_total, bucket)
    returned = lax.all_to_all(outgoing, "tile", split_axis=1, concat_axis=1, tiled=True)
    surface = lax.dot_general(
        returned.reshape(STEPS, slot_total),
        routing_matrix,
        (((1,), (1,)), ((), ())),
        preferred_element_type=jnp.float32,
    )
    surface_accel = surface.astype(jnp.bfloat16).reshape(1, 1, 1, STEPS, slot_total)
    return (final_field, prior_field, surface_accel, modal_state)


def solution(mesh):
    in_specs = (
        P(("groups", "tile"), "sub", "rep"),
        P(("groups", "tile"), "sub", "rep"),
        P(("groups", "tile"), "sub", "rep"),
        P(("groups", "tile", "sub", "rep")),
        P(("groups", "tile", "sub", "rep"), None),
        P("groups"),
        P("groups"),
        P(None, "groups"),
        P(("groups", "tile"), "sub", "rep", None),
        P(("groups", "tile"), "sub", "rep", None, None),
        P(("groups", "sub"), "rep", "tile"),
    )
    out_specs = (
        P(("groups", "tile"), "sub", "rep"),
        P(("groups", "tile"), "sub", "rep"),
        P(("groups", "tile"), "sub", "rep", None, None),
        P(None, ("groups", "tile", "sub", "rep")),
    )
    return jax.shard_map(body, mesh=mesh, in_specs=in_specs, out_specs=out_specs, check_vma=False)
```

profile of v0, /device:TPU:0, one launch (start us, length us, event | category | flops | bytes accessed | tf_op | source)
XLA Modules:
  0.0 172.1 jit_solution(446253793117891918)
XLA Ops:
  7.2 0.9 fusion.41
  8.1 5.0 %collective-permute-start = (f32[2,4,16,128]{3,2,1,0:T(8,128)S(1)}, f32[2,4,16,128]{3,2,1,0:T(8,128)S(1)}, u32[]{:S(2)}, u32[]{:S(2)}) collective-permute-start(f32[2,4,16,128]{3,2,1,0:T(8,128)S(1)} %get-tuple-element.142), channel_id=1, source_target_pairs={{0,4},{4,8},{8,12},{1,5},{5,9},{9,13},{2,6},{6,10},{10,14},{3,7},{... | collective-permute-start | bytes 196616 | tf_op jit(solution)/shard_map/while/body/eval_jaxpr/ppermute | solution.py:19
  13.1 1.3 collective-permute-start.1
  15.2 4.5 %collective-permute-start.6 = (f32[4,16,128]{2,1,0:T(8,128)S(1)}, f32[4,16,128]{2,1,0:T(8,128)S(1)}, u32[]{:S(2)}, u32[]{:S(2)}) collective-permute-start(f32[4,16,128]{2,1,0:T(8,128)S(1)} %get-tuple-element.145), channel_id=1, source_target_pairs={{0,4},{4,8},{8,12},{1,5},{5,9},{9,13},{2,6},{6,10},{10,14},{3,7},{... | collective-permute-start | bytes 98312 | tf_op jit(solution)/shard_map/ppermute | solution.py:19
  19.7 1.3 collective-permute-start.7
  24.3 0.8 constant_dynamic-update-slice_fusion.1
  25.6 3.4 %collective-permute-start.8 = (f32[16,4,128]{2,1,0:T(4,128)S(1)}, f32[16,4,128]{2,1,0:T(4,128)S(1)}, u32[]{:S(2)}, u32[]{:S(2)}) collective-permute-start(f32[16,4,128]{2,1,0:T(4,128)S(1)} %get-tuple-element.140), channel_id=1, source_target_pairs={{0,2},{1,3},{4,6},{5,7},{8,10},{9,11},{12,14},{13,15},{16,18},{17,... | collective-permute-start | bytes 98312 | tf_op jit(solution)/shard_map/ppermute | solution.py:19
  29.0 1.3 collective-permute-start.9
  31.1 4.5 %collective-permute-start.2 = (f32[2,16,4,128]{3,2,1,0:T(4,128)S(1)}, f32[2,16,4,128]{3,2,1,0:T(4,128)S(1)}, u32[]{:S(2)}, u32[]{:S(2)}) collective-permute-start(f32[2,16,4,128]{3,2,1,0:T(4,128)S(1)} %get-tuple-element.136), channel_id=1, source_target_pairs={{0,2},{1,3},{4,6},{5,7},{8,10},{9,11},{12,14},{13,15},{16,18},{17,... | collective-permute-start | bytes 196616 | tf_op jit(solution)/shard_map/while/body/eval_jaxpr/ppermute | solution.py:19
  35.7 1.3 collective-permute-start.3
  37.2 1.3 collective-permute-start.10
  38.5 1.3 collective-permute-start.11
  39.8 2.1 %collective-permute-done.3 = f32[2,16,4,128]{3,2,1,0:T(4,128)S(1)} collective-permute-done((f32[2,16,4,128]{3,2,1,0:T(4,128)S(1)}, f32[2,16,4,128]{3,2,1,0:T(4,128)S(1)}, u32[]{:S(2)}, u32[]{:S(2)}) %collective-permute-start.3) | collective-permute-done | bytes 65568 | tf_op jit(solution)/shard_map/while/body/eval_jaxpr/ppermute | solution.py:20
  42.1 1.3 collective-permute-start.4
  43.4 1.3 collective-permute-start.5
  45.1 2.0 %collective-permute-done.5 = f32[2,16,24,4]{3,2,1,0:T(8,128)S(1)} collective-permute-done((f32[2,16,24,4]{3,2,1,0:T(8,128)S(1)}, f32[2,16,24,4]{3,2,1,0:T(8,128)S(1)}, u32[]{:S(2)}, u32[]{:S(2)}) %collective-permute-start.5) | collective-permute-done | bytes 12320 | tf_op jit(solution)/shard_map/while/body/eval_jaxpr/ppermute | solution.py:20
  47.7 1.4 slice_subtract_fusion
  49.2 1.2 slice_subtract_fusion.1
  50.5 1.0 slice_subtract_fusion.2
  51.9 2.5 %gather_fusion.2 = bf16[384]{0:T(512)(128)(2,1)S(1)} fusion(f32[16384]{0:T(1024)S(1)} %bitcast.42, s32[1024]{0:T(1024)S(1)} %pad_clamp_fusion), kind=kCustom, calls=%fused_computation.2.clone | custom fusion | bytes 3072 | tf_op jit(solution)/shard_map/while/body/eval_jaxpr/jit(_take)/gather | solution.py:130
  54.5 2.5 %gather_fusion.3 = bf16[384]{0:T(512)(128)(2,1)S(1)} fusion(f32[16384]{0:T(1024)S(1)} %bitcast.41, s32[1024]{0:T(1024)S(1)} %pad_clamp_fusion), kind=kCustom, calls=%fused_computation.3.clone | custom fusion | bytes 3072 | tf_op jit(solution)/shard_map/while/body/eval_jaxpr/jit(_take)/gather | solution.py:130
  57.0 2.8 %gather_fusion.1 = bf16[384]{0:T(512)(128)(2,1)S(1)} fusion(bf16[16384]{0:T(1024)(128)(2,1)S(1)} %bitcast.40, s32[1024]{0:T(1024)S(1)} %pad_clamp_fusion), kind=kCustom, calls=%fused_computation.1.clone | custom fusion | bytes 3072 | tf_op jit(solution)/shard_map/while/body/eval_jaxpr/jit(_take)/gather | solution.py:130
  59.9 2.8 %gather_fusion = bf16[384]{0:T(512)(128)(2,1)S(1)} fusion(bf16[16384]{0:T(1024)(128)(2,1)S(1)} %bitcast.39, s32[1024]{0:T(1024)S(1)} %pad_clamp_fusion), kind=kCustom, calls=%fused_computation.clone | custom fusion | bytes 3072 | tf_op jit(solution)/shard_map/while/body/eval_jaxpr/jit(_take)/gather | solution.py:130
  63.7 5.5 %all-to-all-start = ((bf16[4,4,96]{2,0,1:T(4,128)(2,1)}), bf16[4,4,96]{2,0,1:T(4,128)(2,1)S(1)}, u32[]{:S(2)}, u32[]{:S(2)}) async-start(bf16[4,4,96]{2,0,1:T(4,128)(2,1)} %copy.17), calls=%async_computation | async-start | bytes 8192 | tf_op jit(solution)/shard_map/all_to_all | solution.py:142
  69.3 5.6 %all-to-all-done = bf16[4,4,96]{2,0,1:T(4,128)(2,1)S(1)} async-done(((bf16[4,4,96]{2,0,1:T(4,128)(2,1)}), bf16[4,4,96]{2,0,1:T(4,128)(2,1)S(1)}, u32[]{:S(2)}, u32[]{:S(2)}) %all-to-all-start) | async-done | bytes 3104 | tf_op jit(solution)/shard_map/all_to_all | solution.py:142
  75.0 1.7 %convolution_bitcast_fusion = f32[2048,4]{1,0:T(8,128)} fusion(bf16[384,2048]{1,0:T(8,128)(2,1)S(1)} %copy-done, f32[4,384]{1,0:T(4,128)S(1)} %reshape.139, f32[384]{0:T(512)S(1)} %copy-done.6), kind=kOutput, calls=%fused_computation.6 | convolution fusion | flops 6294528 | bytes 1613312
  78.3 55.4 %reduce-scatter.4.cloned.1.call-done = f32[128,4]{1,0:T(8,128)} async-done(((f32[2048,4]{1,0:T(8,128)}), f32[128,4]{1,0:T(8,128)}) %reduce-scatter.4.cloned.1.call-update) | async-done | bytes 2064
  133.7 0.9 copy.22
  134.9 19.4 %all_gather.3 = bf16[4,2048]{1,0:T(4,128)(2,1)S(1)} all-gather(bf16[4,128]{1,0:T(4,128)(2,1)S(1)} %get-tuple-element.98), channel_id=1, replica_groups=mesh['groups'=2,'tile'=4,'sub'=2,'rep'=2] {'tile','sub','rep'}, dimensions={1}, use_global_device_ids=true | all-gather | bytes 17408 | tf_op jit(solution)/shard_map/all_gather | solution.py:159
  155.5 3.2 %all-to-all-start.1 = ((bf16[4,4,96]{2,0,1:T(4,128)(2,1)}), bf16[4,4,96]{2,0,1:T(4,128)(2,1)S(1)}, u32[]{:S(2)}, u32[]{:S(2)}) async-start(bf16[4,4,96]{2,0,1:T(4,128)(2,1)} %copy.19), calls=%async_computation.1 | async-start | bytes 8192 | tf_op jit(solution)/shard_map/all_to_all | solution.py:165
  159.3 5.0 %all-to-all-done.1 = bf16[4,4,96]{2,0,1:T(4,128)(2,1)S(1)} async-done(((bf16[4,4,96]{2,0,1:T(4,128)(2,1)}), bf16[4,4,96]{2,0,1:T(4,128)(2,1)S(1)}, u32[]{:S(2)}, u32[]{:S(2)}) %all-to-all-start.1) | async-done | bytes 3104 | tf_op jit(solution)/shard_map/all_to_all | solution.py:165
  164.4 0.9 fusion.2
  (85 shorter events, 11.5 us)
Async XLA Ops:
  7.2 67.8 %copy-start = (bf16[384,2048]{1,0:T(8,128)(2,1)S(1)}, bf16[384,2048]{1,0:T(8,128)(2,1)}, u32[]{:S(2)}) copy-start(bf16[384,2048]{1,0:T(8,128)(2,1)} %param.19) | copy-start | bytes 4718596
  7.2 34.7 %copy-start.3 = (f32[8,16,128]{2,1,0:T(8,128)S(1)}, f32[8,16,128]{2,1,0:T(8,128)}, u32[]{:S(2)}) copy-start(f32[8,16,128]{2,1,0:T(8,128)} %param.15) | copy-start | bytes 196612
  7.2 34.7 %copy-start.4 = (f32[8,16,128]{2,1,0:T(8,128)S(1)}, f32[8,16,128]{2,1,0:T(8,128)}, u32[]{:S(2)}) copy-start(f32[8,16,128]{2,1,0:T(8,128)} %param.16) | copy-start | bytes 196612
  8.1 22.1 %collective-permute-start = (f32[2,4,16,128]{3,2,1,0:T(8,128)S(1)}, f32[2,4,16,128]{3,2,1,0:T(8,128)S(1)}, u32[]{:S(2)}, u32[]{:S(2)}) collective-permute-start(f32[2,4,16,128]{3,2,1,0:T(8,128)S(1)} %get-tuple-element.142), channel_id=1, source_target_pairs={{0,4},{4,8},{8,12},{1,5},{5,9},{9,13},{2,6},{6,10},{10,14},{3,7},{... | collective-permute-start | bytes 196616 | tf_op jit(solution)/shard_map/while/body/eval_jaxpr/ppermute | solution.py:19
  13.1 17.2 %collective-permute-start.1 = (f32[2,4,16,128]{3,2,1,0:T(8,128)S(1)}, f32[2,4,16,128]{3,2,1,0:T(8,128)S(1)}, u32[]{:S(2)}, u32[]{:S(2)}) collective-permute-start(f32[2,4,16,128]{3,2,1,0:T(8,128)S(1)} %get-tuple-element.143), channel_id=1, source_target_pairs={{4,0},{8,4},{12,8},{5,1},{9,5},{13,9},{6,2},{10,6},{14,10},{7,3},{... | collective-permute-start | bytes 196616 | tf_op jit(solution)/shard_map/while/body/eval_jaxpr/ppermute | solution.py:20
  15.2 9.1 %collective-permute-start.6 = (f32[4,16,128]{2,1,0:T(8,128)S(1)}, f32[4,16,128]{2,1,0:T(8,128)S(1)}, u32[]{:S(2)}, u32[]{:S(2)}) collective-permute-start(f32[4,16,128]{2,1,0:T(8,128)S(1)} %get-tuple-element.145), channel_id=1, source_target_pairs={{0,4},{4,8},{8,12},{1,5},{5,9},{9,13},{2,6},{6,10},{10,14},{3,7},{... | collective-permute-start | bytes 98312 | tf_op jit(solution)/shard_map/ppermute | solution.py:19
  19.7 5.8 %collective-permute-start.7 = (f32[4,16,128]{2,1,0:T(8,128)S(1)}, f32[4,16,128]{2,1,0:T(8,128)S(1)}, u32[]{:S(2)}, u32[]{:S(2)}) collective-permute-start(f32[4,16,128]{2,1,0:T(8,128)S(1)} %get-tuple-element.144), channel_id=1, source_target_pairs={{4,0},{8,4},{12,8},{5,1},{9,5},{13,9},{6,2},{10,6},{14,10},{7,3},{... | collective-permute-start | bytes 98312 | tf_op jit(solution)/shard_map/ppermute | solution.py:20
  25.6 11.4 %collective-permute-start.8 = (f32[16,4,128]{2,1,0:T(4,128)S(1)}, f32[16,4,128]{2,1,0:T(4,128)S(1)}, u32[]{:S(2)}, u32[]{:S(2)}) collective-permute-start(f32[16,4,128]{2,1,0:T(4,128)S(1)} %get-tuple-element.140), channel_id=1, source_target_pairs={{0,2},{1,3},{4,6},{5,7},{8,10},{9,11},{12,14},{13,15},{16,18},{17,... | collective-permute-start | bytes 98312 | tf_op jit(solution)/shard_map/ppermute | solution.py:19
  29.0 8.0 %collective-permute-start.9 = (f32[16,4,128]{2,1,0:T(4,128)S(1)}, f32[16,4,128]{2,1,0:T(4,128)S(1)}, u32[]{:S(2)}, u32[]{:S(2)}) collective-permute-start(f32[16,4,128]{2,1,0:T(4,128)S(1)} %get-tuple-element.141), channel_id=1, source_target_pairs={{2,0},{3,1},{6,4},{7,5},{10,8},{11,9},{14,12},{15,13},{18,16},{19,... | collective-permute-start | bytes 98312 | tf_op jit(solution)/shard_map/ppermute | solution.py:20
  31.1 8.6 %collective-permute-start.2 = (f32[2,16,4,128]{3,2,1,0:T(4,128)S(1)}, f32[2,16,4,128]{3,2,1,0:T(4,128)S(1)}, u32[]{:S(2)}, u32[]{:S(2)}) collective-permute-start(f32[2,16,4,128]{3,2,1,0:T(4,128)S(1)} %get-tuple-element.136), channel_id=1, source_target_pairs={{0,2},{1,3},{4,6},{5,7},{8,10},{9,11},{12,14},{13,15},{16,18},{17,... | collective-permute-start | bytes 196616 | tf_op jit(solution)/shard_map/while/body/eval_jaxpr/ppermute | solution.py:19
  35.7 6.2 %collective-permute-start.3 = (f32[2,16,4,128]{3,2,1,0:T(4,128)S(1)}, f32[2,16,4,128]{3,2,1,0:T(4,128)S(1)}, u32[]{:S(2)}, u32[]{:S(2)}) collective-permute-start(f32[2,16,4,128]{3,2,1,0:T(4,128)S(1)} %get-tuple-element.137), channel_id=1, source_target_pairs={{2,0},{3,1},{6,4},{7,5},{10,8},{11,9},{14,12},{15,13},{18,16},{19,... | collective-permute-start | bytes 196616 | tf_op jit(solution)/shard_map/while/body/eval_jaxpr/ppermute | solution.py:20
  37.2 7.6 %collective-permute-start.10 = (f32[16,24,4]{2,1,0:T(8,128)S(1)}, f32[16,24,4]{2,1,0:T(8,128)S(1)}, u32[]{:S(2)}, u32[]{:S(2)}) collective-permute-start(f32[16,24,4]{2,1,0:T(8,128)S(1)} %get-tuple-element.138), channel_id=1, source_target_pairs={{0,1},{2,3},{4,5},{6,7},{8,9},{10,11},{12,13},{14,15},{16,17},{18,... | collective-permute-start | bytes 18440 | tf_op jit(solution)/shard_map/ppermute | solution.py:19
  38.5 6.3 %collective-permute-start.11 = (f32[16,24,4]{2,1,0:T(8,128)S(1)}, f32[16,24,4]{2,1,0:T(8,128)S(1)}, u32[]{:S(2)}, u32[]{:S(2)}) collective-permute-start(f32[16,24,4]{2,1,0:T(8,128)S(1)} %get-tuple-element.139), channel_id=1, source_target_pairs={{1,0},{3,2},{5,4},{7,6},{9,8},{11,10},{13,12},{15,14},{17,16},{19,... | collective-permute-start | bytes 18440 | tf_op jit(solution)/shard_map/ppermute | solution.py:20
  42.1 2.9 %collective-permute-start.4 = (f32[2,16,24,4]{3,2,1,0:T(8,128)S(1)}, f32[2,16,24,4]{3,2,1,0:T(8,128)S(1)}, u32[]{:S(2)}, u32[]{:S(2)}) collective-permute-start(f32[2,16,24,4]{3,2,1,0:T(8,128)S(1)} %get-tuple-element.134), channel_id=1, source_target_pairs={{0,1},{2,3},{4,5},{6,7},{8,9},{10,11},{12,13},{14,15},{16,17},{18,... | collective-permute-start | bytes 36872 | tf_op jit(solution)/shard_map/while/body/eval_jaxpr/ppermute | solution.py:19
  43.4 3.6 %collective-permute-start.5 = (f32[2,16,24,4]{3,2,1,0:T(8,128)S(1)}, f32[2,16,24,4]{3,2,1,0:T(8,128)S(1)}, u32[]{:S(2)}, u32[]{:S(2)}) collective-permute-start(f32[2,16,24,4]{3,2,1,0:T(8,128)S(1)} %get-tuple-element.135), channel_id=1, source_target_pairs={{1,0},{3,2},{5,4},{7,6},{9,8},{11,10},{13,12},{15,14},{17,16},{19,... | collective-permute-start | bytes 36872 | tf_op jit(solution)/shard_map/while/body/eval_jaxpr/ppermute | solution.py:20
  50.5 1.1 copy-start.5
  51.9 7.9 %copy-start.1 = (f32[8,16,128]{2,1,0:T(8,128)}, f32[8,16,128]{2,1,0:T(8,128)S(1)}, u32[]{:S(2)}) copy-start(f32[8,16,128]{2,1,0:T(8,128)S(1)} %get-tuple-element.124) | copy-start | bytes 196612
  51.9 7.9 %copy-start.2 = (f32[8,16,128]{2,1,0:T(8,128)}, f32[8,16,128]{2,1,0:T(8,128)S(1)}, u32[]{:S(2)}) copy-start(f32[8,16,128]{2,1,0:T(8,128)S(1)} %get-tuple-element.125) | copy-start | bytes 196612
  54.5 20.5 %copy-start.6 = (f32[384]{0:T(512)S(1)}, f32[384]{0:T(512)}, u32[]{:S(2)}) copy-start(f32[384]{0:T(512)} %param.18) | copy-start | bytes 4612
  63.7 11.1 %all-to-all-start = ((bf16[4,4,96]{2,0,1:T(4,128)(2,1)}), bf16[4,4,96]{2,0,1:T(4,128)(2,1)S(1)}, u32[]{:S(2)}, u32[]{:S(2)}) async-start(bf16[4,4,96]{2,0,1:T(4,128)(2,1)} %copy.17), calls=%async_computation | async-start | bytes 8192 | tf_op jit(solution)/shard_map/all_to_all | solution.py:142
  69.3 64.4 %reduce-scatter.4.cloned.1.call-start = ((), (), s32[]{:S(2)}) async-start(), calls=%async_computation.3 | async-start | bytes 1114112
  155.5 8.8 %all-to-all-start.1 = ((bf16[4,4,96]{2,0,1:T(4,128)(2,1)}), bf16[4,4,96]{2,0,1:T(4,128)(2,1)S(1)}, u32[]{:S(2)}, u32[]{:S(2)}) async-start(bf16[4,4,96]{2,0,1:T(4,128)(2,1)} %copy.19), calls=%async_computation.1 | async-start | bytes 8192 | tf_op jit(solution)/shard_map/all_to_all | solution.py:165
Sparse Core Ops, SparseCore 0:
  76.9 56.7 reduce-scatter.3
where the time goes:
time: 173 us; the launch traced here: 172 us
  waiting for transfers between devices  70.5 us (41%)
  starting transfers between devices  36.6 us (21%)
  blocking collectives  19.4 us (11%)
  local copies, waits for them, and re-layouts  17 us (10%)
  between operations  15.2 us (9%)
  other arithmetic  9.79 us (6%)
  matrix products  3.65 us (2%)
    unnamed x2, waiting for transfers between devices  55.5 us
    ppermute x6, starting transfers between devices, extended(): before = lax.ppermute(last, axis, up)  20.1 us
    all_gather x1, blocking collectives, body(): lax.all_gather(modal_rounded, ('tile', 'sub', 'rep'), axis=1, tiled=True)  19.4 us
    gather x4, local copies, waits for them, and re-layouts, deep_block(): jnp.take(interior.reshape(-1), cell_index).astype(jnp.bfloat16)  10.7 us
    ppermute x6, starting transfers between devices, extended(): after = lax.ppermute(first, axis, down)  7.75 us
    all_to_all x1, waiting for transfers between devices, body(): lax.all_to_all(bucketed, 'tile', split_axis=1, concat_axis=1, tiled=True)  5.57 us
    all_to_all x1, starting transfers between devices, body(): lax.all_to_all(bucketed, 'tile', split_axis=1, concat_axis=1, tiled=True)  5.54 us
    all_to_all x1, waiting for transfers between devices, body(): lax.all_to_all(outgoing, 'tile', split_axis=1, concat_axis=1, tiled=True)  4.98 us
  transfers between devices with their start and end apart: 15, of which 6 were waited for; matrix products, arithmetic and copies ran while one was open for 5% of the time, Pallas kernels for 0%

commit v1 on v0

--- a/solution.py
+++ b/solution.py
@@ -7,6 +7,11 @@
 HALO = 4
 nonlinear = 0.03
 viscous = 0.02
+
+
+def gather_blocks(x, axis, dim):
+    parts = lax.all_gather(x, axis)
+    return jnp.concatenate(parts, axis=dim)
 
 
 def extended(shard, sides, width):
@@ -156,7 +161,7 @@
     modal_accel, modal_state = oscillate(forces, local_frequency, local_damping, local_start)
     modal_rounded = modal_accel.astype(jnp.bfloat16)
     node_accel = lax.dot_general(
-        lax.all_gather(modal_rounded, ("tile", "sub", "rep"), axis=1, tiled=True),
+        gather_blocks(modal_rounded, ("tile", "sub", "rep"), 1),
         mode_shapes,
         (((1,), (1,)), ((), ())),
         preferred_element_type=jnp.float32,

time: 173 us -> 173 us (level)
  no operation moved by 1% of the time
where the time goes in v1:
time: 173 us; the launch traced here: 172 us
  waiting for transfers between devices  70.5 us (41%)
  starting transfers between devices  36.6 us (21%)
  blocking collectives  19.4 us (11%)
  local copies, waits for them, and re-layouts  17 us (10%)
  between operations  15.2 us (9%)
  other arithmetic  9.79 us (6%)
  matrix products  3.65 us (2%)
    unnamed x2, waiting for transfers between devices  55.5 us
    ppermute x6, starting transfers between devices, extended(): before = lax.ppermute(last, axis, up)  20.1 us
    all_gather x1, blocking collectives, gather_blocks(): parts = lax.all_gather(x, axis)  19.4 us
    gather x4, local copies, waits for them, and re-layouts, deep_block(): jnp.take(interior.reshape(-1), cell_index).astype(jnp.bfloat16)  10.7 us
    ppermute x6, starting transfers between devices, extended(): after = lax.ppermute(first, axis, down)  7.75 us
    all_to_all x1, waiting for transfers between devices, body(): lax.all_to_all(bucketed, 'tile', split_axis=1, concat_axis=1, tiled=True)  5.57 us
    all_to_all x1, starting transfers between devices, body(): lax.all_to_all(bucketed, 'tile', split_axis=1, concat_axis=1, tiled=True)  5.54 us
    all_to_all x1, waiting for transfers between devices, body(): lax.all_to_all(outgoing, 'tile', split_axis=1, concat_axis=1, tiled=True)  4.98 us
  transfers between devices with their start and end apart: 15, of which 6 were waited for; matrix products, arithmetic and copies ran while one was open for 5% of the time, Pallas kernels for 0%

profile of v1, /device:TPU:0, one launch (start us, length us, event | category | flops | bytes accessed | tf_op | source)
XLA Modules:
  0.0 172.1 jit_solution(18394078761567606620)
XLA Ops:
  7.2 0.9 fusion.41
  8.1 5.0 %collective-permute-start = (f32[2,4,16,128]{3,2,1,0:T(8,128)S(1)}, f32[2,4,16,128]{3,2,1,0:T(8,128)S(1)}, u32[]{:S(2)}, u32[]{:S(2)}) collective-permute-start(f32[2,4,16,128]{3,2,1,0:T(8,128)S(1)} %get-tuple-element.142), channel_id=1, source_target_pairs={{0,4},{4,8},{8,12},{1,5},{5,9},{9,13},{2,6},{6,10},{10,14},{3,7},{... | collective-permute-start | bytes 196616 | tf_op jit(solution)/shard_map/while/body/eval_jaxpr/ppermute | solution.py:24
  13.1 1.3 collective-permute-start.1
  15.2 4.5 %collective-permute-start.6 = (f32[4,16,128]{2,1,0:T(8,128)S(1)}, f32[4,16,128]{2,1,0:T(8,128)S(1)}, u32[]{:S(2)}, u32[]{:S(2)}) collective-permute-start(f32[4,16,128]{2,1,0:T(8,128)S(1)} %get-tuple-element.145), channel_id=1, source_target_pairs={{0,4},{4,8},{8,12},{1,5},{5,9},{9,13},{2,6},{6,10},{10,14},{3,7},{... | collective-permute-start | bytes 98312 | tf_op jit(solution)/shard_map/ppermute | solution.py:24
  19.7 1.3 collective-permute-start.7
  24.3 0.8 constant_dynamic-update-slice_fusion.1
  25.6 3.4 %collective-permute-start.8 = (f32[16,4,128]{2,1,0:T(4,128)S(1)}, f32[16,4,128]{2,1,0:T(4,128)S(1)}, u32[]{:S(2)}, u32[]{:S(2)}) collective-permute-start(f32[16,4,128]{2,1,0:T(4,128)S(1)} %get-tuple-element.140), channel_id=1, source_target_pairs={{0,2},{1,3},{4,6},{5,7},{8,10},{9,11},{12,14},{13,15},{16,18},{17,... | collective-permute-start | bytes 98312 | tf_op jit(solution)/shard_map/ppermute | solution.py:24
  29.0 1.3 collective-permute-start.9
  31.1 4.5 %collective-permute-start.2 = (f32[2,16,4,128]{3,2,1,0:T(4,128)S(1)}, f32[2,16,4,128]{3,2,1,0:T(4,128)S(1)}, u32[]{:S(2)}, u32[]{:S(2)}) collective-permute-start(f32[2,16,4,128]{3,2,1,0:T(4,128)S(1)} %get-tuple-element.136), channel_id=1, source_target_pairs={{0,2},{1,3},{4,6},{5,7},{8,10},{9,11},{12,14},{13,15},{16,18},{17,... | collective-permute-start | bytes 196616 | tf_op jit(solution)/shard_map/while/body/eval_jaxpr/ppermute | solution.py:24
  35.7 1.3 collective-permute-start.3
  37.2 1.3 collective-permute-start.10
  38.5 1.3 collective-permute-start.11
  39.8 2.1 %collective-permute-done.3 = f32[2,16,4,128]{3,2,1,0:T(4,128)S(1)} collective-permute-done((f32[2,16,4,128]{3,2,1,0:T(4,128)S(1)}, f32[2,16,4,128]{3,2,1,0:T(4,128)S(1)}, u32[]{:S(2)}, u32[]{:S(2)}) %collective-permute-start.3) | collective-permute-done | bytes 65568 | tf_op jit(solution)/shard_map/while/body/eval_jaxpr/ppermute | solution.py:25
  42.1 1.3 collective-permute-start.4
  43.4 1.3 collective-permute-start.5
  45.1 2.0 %collective-permute-done.5 = f32[2,16,24,4]{3,2,1,0:T(8,128)S(1)} collective-permute-done((f32[2,16,24,4]{3,2,1,0:T(8,128)S(1)}, f32[2,16,24,4]{3,2,1,0:T(8,128)S(1)}, u32[]{:S(2)}, u32[]{:S(2)}) %collective-permute-start.5) | collective-permute-done | bytes 12320 | tf_op jit(solution)/shard_map/while/body/eval_jaxpr/ppermute | solution.py:25
  47.7 1.4 slice_subtract_fusion
  49.2 1.2 slice_subtract_fusion.1
  50.5 1.0 slice_subtract_fusion.2
  51.9 2.5 %gather_fusion.2 = bf16[384]{0:T(512)(128)(2,1)S(1)} fusion(f32[16384]{0:T(1024)S(1)} %bitcast.49, s32[1024]{0:T(1024)S(1)} %pad_clamp_fusion), kind=kCustom, calls=%fused_computation.2.clone | custom fusion | bytes 3072 | tf_op jit(solution)/shard_map/while/body/eval_jaxpr/jit(_take)/gather | solution.py:135
  54.5 2.5 %gather_fusion.3 = bf16[384]{0:T(512)(128)(2,1)S(1)} fusion(f32[16384]{0:T(1024)S(1)} %bitcast.48, s32[1024]{0:T(1024)S(1)} %pad_clamp_fusion), kind=kCustom, calls=%fused_computation.3.clone | custom fusion | bytes 3072 | tf_op jit(solution)/shard_map/while/body/eval_jaxpr/jit(_take)/gather | solution.py:135
  57.0 2.8 %gather_fusion.1 = bf16[384]{0:T(512)(128)(2,1)S(1)} fusion(bf16[16384]{0:T(1024)(128)(2,1)S(1)} %bitcast.47, s32[1024]{0:T(1024)S(1)} %pad_clamp_fusion), kind=kCustom, calls=%fused_computation.1.clone | custom fusion | bytes 3072 | tf_op jit(solution)/shard_map/while/body/eval_jaxpr/jit(_take)/gather | solution.py:135
  59.9 2.8 %gather_fusion = bf16[384]{0:T(512)(128)(2,1)S(1)} fusion(bf16[16384]{0:T(1024)(128)(2,1)S(1)} %bitcast.46, s32[1024]{0:T(1024)S(1)} %pad_clamp_fusion), kind=kCustom, calls=%fused_computation.clone | custom fusion | bytes 3072 | tf_op jit(solution)/shard_map/while/body/eval_jaxpr/jit(_take)/gather | solution.py:135
  63.7 5.5 %all-to-all-start = ((bf16[4,4,96]{2,0,1:T(4,128)(2,1)}), bf16[4,4,96]{2,0,1:T(4,128)(2,1)S(1)}, u32[]{:S(2)}, u32[]{:S(2)}) async-start(bf16[4,4,96]{2,0,1:T(4,128)(2,1)} %copy.17), calls=%async_computation | async-start | bytes 8192 | tf_op jit(solution)/shard_map/all_to_all | solution.py:147
  69.3 5.6 %all-to-all-done = bf16[4,4,96]{2,0,1:T(4,128)(2,1)S(1)} async-done(((bf16[4,4,96]{2,0,1:T(4,128)(2,1)}), bf16[4,4,96]{2,0,1:T(4,128)(2,1)S(1)}, u32[]{:S(2)}, u32[]{:S(2)}) %all-to-all-start) | async-done | bytes 3104 | tf_op jit(solution)/shard_map/all_to_all | solution.py:147
  75.0 1.7 %convolution_bitcast_fusion = f32[2048,4]{1,0:T(8,128)} fusion(bf16[384,2048]{1,0:T(8,128)(2,1)S(1)} %copy-done, f32[4,384]{1,0:T(4,128)S(1)} %reshape.147, f32[384]{0:T(512)S(1)} %copy-done.6), kind=kOutput, calls=%fused_computation.6 | convolution fusion | flops 6294528 | bytes 1613312
  78.3 55.4 %reduce-scatter.4.cloned.1.call-done = f32[128,4]{1,0:T(8,128)} async-done(((f32[2048,4]{1,0:T(8,128)}), f32[128,4]{1,0:T(8,128)}) %reduce-scatter.4.cloned.1.call-update) | async-done | bytes 2064
  133.7 0.9 copy.22
  134.9 19.4 %all-gather.1 = bf16[16,4,128]{2,1,0:T(4,128)(2,1)S(1)} all-gather(bf16[1,4,128]{2,1,0:T(4,128)(2,1)S(1)} %bitcast.62), channel_id=2, replica_groups=mesh['groups'=2,'tile'=4,'sub'=2,'rep'=2] {'tile','sub','rep'}, dimensions={0}, use_global_device_ids=true | all-gather | bytes 17408 | tf_op jit(solution)/shard_map/all_gather | solution.py:13
  155.5 3.2 %all-to-all-start.1 = ((bf16[4,4,96]{2,0,1:T(4,128)(2,1)}), bf16[4,4,96]{2,0,1:T(4,128)(2,1)S(1)}, u32[]{:S(2)}, u32[]{:S(2)}) async-start(bf16[4,4,96]{2,0,1:T(4,128)(2,1)} %copy.19), calls=%async_computation.1 | async-start | bytes 8192 | tf_op jit(solution)/shard_map/all_to_all | solution.py:170
  159.3 5.0 %all-to-all-done.1 = bf16[4,4,96]{2,0,1:T(4,128)(2,1)S(1)} async-done(((bf16[4,4,96]{2,0,1:T(4,128)(2,1)}), bf16[4,4,96]{2,0,1:T(4,128)(2,1)S(1)}, u32[]{:S(2)}, u32[]{:S(2)}) %all-to-all-start.1) | async-done | bytes 3104 | tf_op jit(solution)/shard_map/all_to_all | solution.py:170
  164.4 0.9 fusion.2
  (85 shorter events, 11.5 us)
Async XLA Ops:
  7.2 67.8 %copy-start = (bf16[384,2048]{1,0:T(8,128)(2,1)S(1)}, bf16[384,2048]{1,0:T(8,128)(2,1)}, u32[]{:S(2)}) copy-start(bf16[384,2048]{1,0:T(8,128)(2,1)} %param.19) | copy-start | bytes 4718596
  7.2 34.7 %copy-start.3 = (f32[8,16,128]{2,1,0:T(8,128)S(1)}, f32[8,16,128]{2,1,0:T(8,128)}, u32[]{:S(2)}) copy-start(f32[8,16,128]{2,1,0:T(8,128)} %param.15) | copy-start | bytes 196612
  7.2 34.7 %copy-start.4 = (f32[8,16,128]{2,1,0:T(8,128)S(1)}, f32[8,16,128]{2,1,0:T(8,128)}, u32[]{:S(2)}) copy-start(f32[8,16,128]{2,1,0:T(8,128)} %param.16) | copy-start | bytes 196612
  8.1 22.1 %collective-permute-start = (f32[2,4,16,128]{3,2,1,0:T(8,128)S(1)}, f32[2,4,16,128]{3,2,1,0:T(8,128)S(1)}, u32[]{:S(2)}, u32[]{:S(2)}) collective-permute-start(f32[2,4,16,128]{3,2,1,0:T(8,128)S(1)} %get-tuple-element.142), channel_id=1, source_target_pairs={{0,4},{4,8},{8,12},{1,5},{5,9},{9,13},{2,6},{6,10},{10,14},{3,7},{... | collective-permute-start | bytes 196616 | tf_op jit(solution)/shard_map/while/body/eval_jaxpr/ppermute | solution.py:24
  13.1 17.2 %collective-permute-start.1 = (f32[2,4,16,128]{3,2,1,0:T(8,128)S(1)}, f32[2,4,16,128]{3,2,1,0:T(8,128)S(1)}, u32[]{:S(2)}, u32[]{:S(2)}) collective-permute-start(f32[2,4,16,128]{3,2,1,0:T(8,128)S(1)} %get-tuple-element.143), channel_id=1, source_target_pairs={{4,0},{8,4},{12,8},{5,1},{9,5},{13,9},{6,2},{10,6},{14,10},{7,3},{... | collective-permute-start | bytes 196616 | tf_op jit(solution)/shard_map/while/body/eval_jaxpr/ppermute | solution.py:25
  15.2 9.1 %collective-permute-start.6 = (f32[4,16,128]{2,1,0:T(8,128)S(1)}, f32[4,16,128]{2,1,0:T(8,128)S(1)}, u32[]{:S(2)}, u32[]{:S(2)}) collective-permute-start(f32[4,16,128]{2,1,0:T(8,128)S(1)} %get-tuple-element.145), channel_id=1, source_target_pairs={{0,4},{4,8},{8,12},{1,5},{5,9},{9,13},{2,6},{6,10},{10,14},{3,7},{... | collective-permute-start | bytes 98312 | tf_op jit(solution)/shard_map/ppermute | solution.py:24
  19.7 5.8 %collective-permute-start.7 = (f32[4,16,128]{2,1,0:T(8,128)S(1)}, f32[4,16,128]{2,1,0:T(8,128)S(1)}, u32[]{:S(2)}, u32[]{:S(2)}) collective-permute-start(f32[4,16,128]{2,1,0:T(8,128)S(1)} %get-tuple-element.144), channel_id=1, source_target_pairs={{4,0},{8,4},{12,8},{5,1},{9,5},{13,9},{6,2},{10,6},{14,10},{7,3},{... | collective-permute-start | bytes 98312 | tf_op jit(solution)/shard_map/ppermute | solution.py:25
  25.6 11.4 %collective-permute-start.8 = (f32[16,4,128]{2,1,0:T(4,128)S(1)}, f32[16,4,128]{2,1,0:T(4,128)S(1)}, u32[]{:S(2)}, u32[]{:S(2)}) collective-permute-start(f32[16,4,128]{2,1,0:T(4,128)S(1)} %get-tuple-element.140), channel_id=1, source_target_pairs={{0,2},{1,3},{4,6},{5,7},{8,10},{9,11},{12,14},{13,15},{16,18},{17,... | collective-permute-start | bytes 98312 | tf_op jit(solution)/shard_map/ppermute | solution.py:24
  29.0 8.0 %collective-permute-start.9 = (f32[16,4,128]{2,1,0:T(4,128)S(1)}, f32[16,4,128]{2,1,0:T(4,128)S(1)}, u32[]{:S(2)}, u32[]{:S(2)}) collective-permute-start(f32[16,4,128]{2,1,0:T(4,128)S(1)} %get-tuple-element.141), channel_id=1, source_target_pairs={{2,0},{3,1},{6,4},{7,5},{10,8},{11,9},{14,12},{15,13},{18,16},{19,... | collective-permute-start | bytes 98312 | tf_op jit(solution)/shard_map/ppermute | solution.py:25
  31.1 8.6 %collective-permute-start.2 = (f32[2,16,4,128]{3,2,1,0:T(4,128)S(1)}, f32[2,16,4,128]{3,2,1,0:T(4,128)S(1)}, u32[]{:S(2)}, u32[]{:S(2)}) collective-permute-start(f32[2,16,4,128]{3,2,1,0:T(4,128)S(1)} %get-tuple-element.136), channel_id=1, source_target_pairs={{0,2},{1,3},{4,6},{5,7},{8,10},{9,11},{12,14},{13,15},{16,18},{17,... | collective-permute-start | bytes 196616 | tf_op jit(solution)/shard_map/while/body/eval_jaxpr/ppermute | solution.py:24
  35.7 6.2 %collective-permute-start.3 = (f32[2,16,4,128]{3,2,1,0:T(4,128)S(1)}, f32[2,16,4,128]{3,2,1,0:T(4,128)S(1)}, u32[]{:S(2)}, u32[]{:S(2)}) collective-permute-start(f32[2,16,4,128]{3,2,1,0:T(4,128)S(1)} %get-tuple-element.137), channel_id=1, source_target_pairs={{2,0},{3,1},{6,4},{7,5},{10,8},{11,9},{14,12},{15,13},{18,16},{19,... | collective-permute-start | bytes 196616 | tf_op jit(solution)/shard_map/while/body/eval_jaxpr/ppermute | solution.py:25
  37.2 7.6 %collective-permute-start.10 = (f32[16,24,4]{2,1,0:T(8,128)S(1)}, f32[16,24,4]{2,1,0:T(8,128)S(1)}, u32[]{:S(2)}, u32[]{:S(2)}) collective-permute-start(f32[16,24,4]{2,1,0:T(8,128)S(1)} %get-tuple-element.138), channel_id=1, source_target_pairs={{0,1},{2,3},{4,5},{6,7},{8,9},{10,11},{12,13},{14,15},{16,17},{18,... | collective-permute-start | bytes 18440 | tf_op jit(solution)/shard_map/ppermute | solution.py:24
  38.5 6.3 %collective-permute-start.11 = (f32[16,24,4]{2,1,0:T(8,128)S(1)}, f32[16,24,4]{2,1,0:T(8,128)S(1)}, u32[]{:S(2)}, u32[]{:S(2)}) collective-permute-start(f32[16,24,4]{2,1,0:T(8,128)S(1)} %get-tuple-element.139), channel_id=1, source_target_pairs={{1,0},{3,2},{5,4},{7,6},{9,8},{11,10},{13,12},{15,14},{17,16},{19,... | collective-permute-start | bytes 18440 | tf_op jit(solution)/shard_map/ppermute | solution.py:25
  42.1 2.9 %collective-permute-start.4 = (f32[2,16,24,4]{3,2,1,0:T(8,128)S(1)}, f32[2,16,24,4]{3,2,1,0:T(8,128)S(1)}, u32[]{:S(2)}, u32[]{:S(2)}) collective-permute-start(f32[2,16,24,4]{3,2,1,0:T(8,128)S(1)} %get-tuple-element.134), channel_id=1, source_target_pairs={{0,1},{2,3},{4,5},{6,7},{8,9},{10,11},{12,13},{14,15},{16,17},{18,... | collective-permute-start | bytes 36872 | tf_op jit(solution)/shard_map/while/body/eval_jaxpr/ppermute | solution.py:24
  43.4 3.6 %collective-permute-start.5 = (f32[2,16,24,4]{3,2,1,0:T(8,128)S(1)}, f32[2,16,24,4]{3,2,1,0:T(8,128)S(1)}, u32[]{:S(2)}, u32[]{:S(2)}) collective-permute-start(f32[2,16,24,4]{3,2,1,0:T(8,128)S(1)} %get-tuple-element.135), channel_id=1, source_target_pairs={{1,0},{3,2},{5,4},{7,6},{9,8},{11,10},{13,12},{15,14},{17,16},{19,... | collective-permute-start | bytes 36872 | tf_op jit(solution)/shard_map/while/body/eval_jaxpr/ppermute | solution.py:25
  50.5 1.1 copy-start.5
  51.9 7.9 %copy-start.1 = (f32[8,16,128]{2,1,0:T(8,128)}, f32[8,16,128]{2,1,0:T(8,128)S(1)}, u32[]{:S(2)}) copy-start(f32[8,16,128]{2,1,0:T(8,128)S(1)} %get-tuple-element.124) | copy-start | bytes 196612
  51.9 7.9 %copy-start.2 = (f32[8,16,128]{2,1,0:T(8,128)}, f32[8,16,128]{2,1,0:T(8,128)S(1)}, u32[]{:S(2)}) copy-start(f32[8,16,128]{2,1,0:T(8,128)S(1)} %get-tuple-element.125) | copy-start | bytes 196612
  54.5 20.5 %copy-start.6 = (f32[384]{0:T(512)S(1)}, f32[384]{0:T(512)}, u32[]{:S(2)}) copy-start(f32[384]{0:T(512)} %param.18) | copy-start | bytes 4612
  63.7 11.1 %all-to-all-start = ((bf16[4,4,96]{2,0,1:T(4,128)(2,1)}), bf16[4,4,96]{2,0,1:T(4,128)(2,1)S(1)}, u32[]{:S(2)}, u32[]{:S(2)}) async-start(bf16[4,4,96]{2,0,1:T(4,128)(2,1)} %copy.17), calls=%async_computation | async-start | bytes 8192 | tf_op jit(solution)/shard_map/all_to_all | solution.py:147
  69.3 64.4 %reduce-scatter.4.cloned.1.call-start = ((), (), s32[]{:S(2)}) async-start(), calls=%async_computation.3 | async-start | bytes 1114112
  155.5 8.8 %all-to-all-start.1 = ((bf16[4,4,96]{2,0,1:T(4,128)(2,1)}), bf16[4,4,96]{2,0,1:T(4,128)(2,1)S(1)}, u32[]{:S(2)}, u32[]{:S(2)}) async-start(bf16[4,4,96]{2,0,1:T(4,128)(2,1)} %copy.19), calls=%async_computation.1 | async-start | bytes 8192 | tf_op jit(solution)/shard_map/all_to_all | solution.py:170
Sparse Core Ops, SparseCore 0:
  76.9 56.7 reduce-scatter.3
